TPU v7x, 512 devices: a whole 4x8x8 slice. The times are simulated.
512 devices in a mesh: wl: 16 (over y, core), sec: 32 (over x, z).
Axes of the slice: x: 4, y: 8, z: 8, core: 2. Of those that a mesh axis runs over, the one named last changes fastest.
Arguments:
- sections: float32 [128, 32, 2, 2, 128, 128], P('sec', None, None, None, 'wl'), as said below
- launch_mode: int32 [32], P('wl'), may hold values from 0 to 127
Outputs:
- forward_field: float32 [128, 32, 2, 128], P('sec', 'wl')
- backward_field: float32 [128, 32, 2, 128], P('sec', 'wl')
Inputs may be any that keep to these rules, and one draw needn't show every extreme that they name: `sections`: every entry is finite; each matrix is a unit-modulus diagonal plus a full coupling, scaled so that it keeps a field's power on average.
All inputs are finite; a program needn't handle non-finite values.
Results may differ from a plain program's by a relative error of at most 0.0003.
Values sent between devices are 32-bit elements; how exact they have to be, the bound alone decides.
No kernel may reach another device: no remote copies, remote signals or barrier semaphores. Data moves between devices by JAX's collectives and lax.ppermute only.
A program may use at most 64 MiB of HBM per device.

v0:
```python
import math
import jax
import jax.numpy as jnp
from jax import lax
from jax.sharding import PartitionSpec as P


def entering(part, axis, combine, identity, reverse):
    count = lax.axis_size(axis)
    place = lax.axis_index(axis)
    ahead = count - 1 - place if reverse else place
    gathered = lax.all_gather(part, axis)
    state = jnp.zeros_like(part) + jnp.asarray(identity, part.dtype)

    def one(turn, state):
        source = count - 1 - turn if reverse else turn
        return combine(state, lax.dynamic_index_in_dim(gathered, source, 0, False))

    return lax.fori_loop(0, ahead, one, state)


def matrix_product(outer_mat, inner_mat):
    return jnp.matmul(outer_mat, inner_mat, precision=lax.Precision.HIGHEST)


def complex_product(outer_mat, inner_mat):
    real_part = matrix_product(outer_mat[..., 0, :, :], inner_mat[..., 0, :, :]) - matrix_product(
        outer_mat[..., 1, :, :], inner_mat[..., 1, :, :]
    )
    imag_part = matrix_product(outer_mat[..., 0, :, :], inner_mat[..., 1, :, :]) + matrix_product(
        outer_mat[..., 1, :, :], inner_mat[..., 0, :, :]
    )
    return jnp.stack([real_part, imag_part], axis=-3)


def complex_apply(matrix, vector):
    real_part = jnp.einsum(
        "...ij,...j->...i", matrix[..., 0, :, :], vector[..., 0, :], precision=lax.Precision.HIGHEST
    ) - jnp.einsum(
        "...ij,...j->...i", matrix[..., 1, :, :], vector[..., 1, :], precision=lax.Precision.HIGHEST
    )
    imag_part = jnp.einsum(
        "...ij,...j->...i", matrix[..., 0, :, :], vector[..., 1, :], precision=lax.Precision.HIGHEST
    ) + jnp.einsum(
        "...ij,...j->...i", matrix[..., 1, :, :], vector[..., 0, :], precision=lax.Precision.HIGHEST
    )
    return jnp.stack([real_part, imag_part], axis=-2)


def combine(earlier, latter):
    return complex_product(latter, earlier)


def shards(sections, launch_mode):
    regrouped = lax.all_to_all(sections, "wl", split_axis=1, concat_axis=4, tiled=True)
    forward_mats = regrouped[:, :, 0]
    backward_mats = regrouped[:, :, 1]
    modes = forward_mats.shape[-1]
    onehot = (jnp.arange(modes)[None, :] == launch_mode[:, None]).astype(jnp.float32) * math.sqrt(
        modes
    )
    launch_field = jnp.stack([onehot, jnp.zeros_like(onehot)], axis=1)

    def extend(running, matrix):
        nxt_mat = complex_product(matrix, running)
        return (nxt_mat, nxt_mat)

    last_forward, later_prefix = lax.scan(extend, forward_mats[0], forward_mats[1:])
    prefixes = jnp.concatenate([forward_mats[:1], later_prefix], axis=0)

    def shrink(running, matrix):
        return (complex_product(matrix, running), running)

    suffix_head, suffix_middle = lax.scan(
        shrink, backward_mats[-1], backward_mats[1:-1], reverse=True
    )
    suffixes = jnp.concatenate([suffix_head[None], suffix_middle], axis=0)
    backward_total = complex_product(backward_mats[0], suffix_head)
    unit_matrix = jnp.eye(modes, dtype=jnp.float32)
    identity_mats = jnp.broadcast_to(
        jnp.stack([unit_matrix, jnp.zeros_like(unit_matrix)], axis=0), last_forward.shape
    )
    forward_before = entering(last_forward, "sec", combine, identity_mats, False)
    backward_after = entering(backward_total, "sec", combine, identity_mats, True)
    entry_field = complex_apply(forward_before, launch_field)
    exit_field = complex_apply(backward_after, launch_field)
    forward_field = complex_apply(prefixes, entry_field)
    backward_field = jnp.concatenate(
        [complex_apply(suffixes, exit_field), exit_field[None]], axis=0
    )
    return (forward_field, backward_field)


def solution(mesh):
    return jax.shard_map(
        shards,
        mesh=mesh,
        in_specs=(P("sec", None, None, None, "wl", None), P("wl")),
        out_specs=(P("sec", "wl", None, None), P("sec", "wl", None, None)),
        check_vma=False,
    )
```

profile of v0, /device:TPU:454, one launch (start us, length us, event | category | flops | bytes accessed | tf_op | source)
XLA Modules:
  0.0 357.5 jit_solution(17075956038594746019)
XLA Ops:
  7.2 3.2 copy.14
  10.3 7.2 %all-to-all-start = ((f32[4,32,2,2,8,128]{5,4,3,2,0,1:T(8,128)}), f32[4,32,2,2,8,128]{5,4,3,2,0,1:T(8,128)S(1)}, u32[]{:S(2)}, u32[]{:S(2)}) async-start(f32[4,32,2,2,8,128]{5,4,3,2,0,1:T(8,128)} %copy.14), calls=%async_computation | async-start | bytes 4194304 | tf_op jit(solution)/shard_map/all_to_all | solution.py:55
  17.6 49.2 %all-to-all-done = f32[4,32,2,2,8,128]{5,4,3,2,0,1:T(8,128)S(1)} async-done(((f32[4,32,2,2,8,128]{5,4,3,2,0,1:T(8,128)}), f32[4,32,2,2,8,128]{5,4,3,2,0,1:T(8,128)S(1)}, u32[]{:S(2)}, u32[]{:S(2)}) %all-to-all-start) | async-done | bytes 2097184 | tf_op jit(solution)/shard_map/all_to_all | solution.py:55
  66.8 1.3 copy-done
  68.1 1.8 copy.75
  71.6 3.9 %while.52 = (s32[]{:T(128)}, f32[2,2,128,128]{3,2,0,1:T(8,128)S(1)}, f32[2,2,2,128,128]{4,3,1,2,0:T(8,128)}, f32[2,2,2,128,128]{4,3,1,2,0:T(8,128)S(1)}, s32[]{:T(128)}) while((s32[]{:T(128)}, f32[2,2,128,128]{3,2,0,1:T(8,128)S(1)}, f32[2,2,2,128,128]{4,3,1,2,0:T(8,128)}, f32[2,2,2,128,128]{4,3,1,2,0:T(8,128)S(1)}, s32[]{:T(128)}) %tuple.105), condition=%wide.region_5.6_spmd, body=%wide.region_4.5_spmd.sunk | while | flops 201457664 | bytes 7602313 | solution.py:74
  78.2 5.6 %while.50 = (s32[]{:T(128)}, f32[2,2,128,128]{3,2,0,1:T(8,128)S(1)}, f32[3,2,2,128,128]{4,3,1,2,0:T(8,128)}, f32[3,2,2,128,128]{4,3,1,2,0:T(8,128)S(1)}, s32[]{:T(128)}) while((s32[]{:T(128)}, f32[2,2,128,128]{3,2,0,1:T(8,128)S(1)}, f32[3,2,2,128,128]{4,3,1,2,0:T(8,128)}, f32[3,2,2,128,128]{4,3,1,2,0:T(8,128)S(1)}, s32[]{:T(128)}) %tuple.99), condition=%wide.region_1.2_spmd, body=%wide.region_0.1_spmd.sunk | while | flops 201457664 | bytes 3145805 | solution.py:68
  84.8 1.2 fusion.51
  86.0 88.7 %all-gather.7.cloned.1.call-done = f32[64,2,128,128]{2,3,0,1:T(8,128)} async-done(((f32[2,2,128,128]{2,3,0,1:T(8,128)}), f32[64,2,128,128]{2,3,0,1:T(8,128)}) %all-gather.7.cloned.1.call-update) | async-done | bytes 8388624 | tf_op jit(solution)/shard_map/all_gather | solution.py:12
  176.0 102.6 %all-gather.5.cloned.1.call-done = f32[64,2,128,128]{3,2,1,0:T(8,128)} async-done(((f32[2,2,128,128]{3,2,1,0:T(8,128)}), f32[64,2,128,128]{3,2,1,0:T(8,128)}) %all-gather.5.cloned.1.call-update) | async-done | bytes 8388624 | tf_op jit(solution)/shard_map/all_gather | solution.py:12
  278.6 65.7 %while.51 = (s32[]{:T(128)}, f32[2,2,128,128]{3,2,0,1:T(8,128)S(1)}, s32[]{:T(128)}, f32[32,2,2,128,128]{4,3,2,1,0:T(8,128)}, s32[]{:T(128)}, /*index=5*/s32[]{:T(128)}, s32[]{:T(128)}) while((s32[]{:T(128)}, f32[2,2,128,128]{3,2,0,1:T(8,128)S(1)}, s32[]{:T(128)}, f32[32,2,2,128,128]{4,3,2,1,0:T(8,128)}, s32[]{:T(128)}, /*index=5*/s32[]{:T(128)}, ...), condition=%wide.region_3.4_spmd, body=%wide.region_2.3_spmd.sunk | while | flops 201457664 | bytes 2883707 | solution.py:19
  278.7 1.0 copy_bitcast_fusion.3
  280.8 1.0 copy_bitcast_fusion.3
  282.9 1.0 copy_bitcast_fusion.3
  285.0 1.0 copy_bitcast_fusion.3
  287.2 1.0 copy_bitcast_fusion.3
  297.8 1.0 copy_bitcast_fusion.3
  308.4 1.0 copy_bitcast_fusion.3
  312.6 1.0 copy_bitcast_fusion.3
  314.7 1.0 copy_bitcast_fusion.3
  323.2 1.0 copy_bitcast_fusion.3
  333.8 1.0 copy_bitcast_fusion.3
  338.0 1.0 copy_bitcast_fusion.3
  340.2 1.0 copy_bitcast_fusion.3
  (270 shorter events, 73.2 us)
Async XLA Ops:
  10.3 56.4 %all-to-all-start = ((f32[4,32,2,2,8,128]{5,4,3,2,0,1:T(8,128)}), f32[4,32,2,2,8,128]{5,4,3,2,0,1:T(8,128)S(1)}, u32[]{:S(2)}, u32[]{:S(2)}) async-start(f32[4,32,2,2,8,128]{5,4,3,2,0,1:T(8,128)} %copy.14), calls=%async_computation | async-start | bytes 4194304 | tf_op jit(solution)/shard_map/all_to_all | solution.py:55
  17.5 157.1 %all-gather.7.cloned.1.call-start = ((), (), s32[]{:S(2)}) async-start(), calls=%async_computation.2 | async-start | bytes 8650752 | tf_op jit(solution)/shard_map/all_gather | solution.py:12
  66.8 1.3 copy-start
  71.6 1.1 copy-start.1
  72.8 0.8 copy-start.2
  73.6 1.1 copy-start.1
  74.8 0.8 copy-start.2
  78.0 200.6 %all-gather.5.cloned.1.call-start = ((), (), s32[]{:S(2)}) async-start(), calls=%async_computation.1 | async-start | bytes 8650752 | tf_op jit(solution)/shard_map/all_gather | solution.py:12
  78.2 6.4 %copy-start.5 = (s32[2]{0:T(128)S(1)}, s32[2]{0:T(128)}, u32[]{:S(2)}) copy-start(s32[2]{0:T(128)} %param.11) | copy-start | bytes 28
  78.2 6.5 %copy-start.3 = (f32[2,2,2,128,128]{4,3,1,2,0:T(8,128)S(1)}, f32[2,2,2,128,128]{4,3,1,2,0:T(8,128)}, u32[]{:S(2)}) copy-start(f32[2,2,2,128,128]{4,3,1,2,0:T(8,128)} %get-tuple-element.194) | copy-start | bytes 1572868
  83.8 1.0 copy-start.4
Sparse Core Ops, SparseCore 0:
  78.2 96.4 all-gather.6
  177.9 100.7 all-gather.4
where the time goes:
time: 359 us; the launch traced here: 358 us
  waiting for transfers between devices  240 us (67%)
  matrix products  46.8 us (13%)
  local copies, waits for them, and re-layouts  40.9 us (11%)
  between operations  14.2 us (4%)
  starting transfers between devices  7.29 us (2%)
  other arithmetic  5.63 us (2%)
    all_gather x2, waiting for transfers between devices, entering(): gathered = lax.all_gather(part, axis)  191 us
    all_to_all x1, waiting for transfers between devices, shards(): lax.all_to_all(sections, 'wl', split_axis=1, concat_axis=4, tiled=True)  49.2 us
    dot_general x148, matrix products, matrix_product(): return jnp.matmul(outer_mat, inner_mat, precision=lax.Precision.HIGHEST)  40 us
    squeeze x31, local copies, waits for them, and re-layouts, one(): return combine(state, lax.dynamic_index_in_dim(gathered, source, 0, False))  30.1 us
    all_to_all x1, starting transfers between devices, shards(): lax.all_to_all(sections, 'wl', split_axis=1, concat_axis=4, tiled=True)  7.21 us
  transfers between devices with their start and end apart: 3, of which 3 were waited for; matrix products, arithmetic and copies ran while one was open for 2% of the time, Pallas kernels for 0%

commit v1 on v0

--- a/solution.py
+++ b/solution.py
@@ -52,7 +52,10 @@
 
 
 def shards(sections, launch_mode):
-    regrouped = lax.all_to_all(sections, "wl", split_axis=1, concat_axis=4, tiled=True)
+    n_dev = lax.axis_size("wl")
+    shards_2 = jnp.stack(jnp.split(sections, n_dev, axis=1), axis=0)
+    shards_2 = lax.all_to_all(shards_2, "wl", split_axis=0, concat_axis=0)
+    regrouped = jnp.concatenate(shards_2, axis=4)
     forward_mats = regrouped[:, :, 0]
     backward_mats = regrouped[:, :, 1]
     modes = forward_mats.shape[-1]

time: 359 us -> 379 us (1.056)
  local copies, waits for them, and re-layouts: 40.9 us -> 61.3 us
    unnamed x9 -> x21, local copies, waits for them, and re-layouts: 4.63 us -> 23.6 us
where the time goes in v1:
time: 379 us; the launch traced here: 378 us
  waiting for transfers between devices  241 us (64%)
  local copies, waits for them, and re-layouts  61.3 us (16%)
  matrix products  46.3 us (12%)
  between operations  14.3 us (4%)
  starting transfers between devices  7.34 us (2%)
  other arithmetic  5.61 us (1%)
    all_gather x2, waiting for transfers between devices, entering(): gathered = lax.all_gather(part, axis)  191 us
    all_to_all x1, waiting for transfers between devices, shards(): shards_2 = lax.all_to_all(shards_2, 'wl', split_axis=0, concat_axis=0)  49.2 us
    dot_general x148, matrix products, matrix_product(): return jnp.matmul(outer_mat, inner_mat, precision=lax.Precision.HIGHEST)  39.5 us
    squeeze x31, local copies, waits for them, and re-layouts, one(): return combine(state, lax.dynamic_index_in_dim(gathered, source, 0, False))  30.1 us
    unnamed x21, local copies, waits for them, and re-layouts  23.6 us
  transfers between devices with their start and end apart: 3, of which 3 were waited for; matrix products, arithmetic and copies ran while one was open for 2% of the time, Pallas kernels for 0%

profile of v1, /device:TPU:454, one launch (start us, length us, event | category | flops | bytes accessed | tf_op | source)
XLA Modules:
  0.0 377.5 jit_solution(12831210185925235947)
XLA Ops:
  7.2 1.6 bitcast_dynamic-update-slice_fusion.17
  8.7 1.6 bitcast_dynamic-update-slice_fusion.16
  10.3 1.6 bitcast_dynamic-update-slice_fusion.15
  11.9 1.6 bitcast_dynamic-update-slice_fusion.14
  13.4 1.6 bitcast_dynamic-update-slice_fusion.13
  15.0 1.6 bitcast_dynamic-update-slice_fusion.12
  16.6 1.6 bitcast_dynamic-update-slice_fusion.11
  18.1 1.6 bitcast_dynamic-update-slice_fusion.10
  19.7 1.6 bitcast_dynamic-update-slice_fusion.9
  21.3 1.6 bitcast_dynamic-update-slice_fusion.8
  22.8 1.6 bitcast_dynamic-update-slice_fusion.7
  24.4 1.6 bitcast_dynamic-update-slice_fusion.6
  25.9 1.6 bitcast_dynamic-update-slice_fusion.5
  27.5 1.6 bitcast_dynamic-update-slice_fusion.4
  29.1 1.6 bitcast_dynamic-update-slice_fusion.3
  30.6 1.6 bitcast_dynamic-update-slice_fusion.2
  32.2 7.3 %all-to-all-start = ((f32[16,4,2,2,2,8,128]{6,5,4,3,2,1,0:T(8,128)}), f32[16,4,2,2,2,8,128]{6,5,4,3,2,1,0:T(8,128)}, u32[]{:S(2)}, u32[]{:S(2)}) async-start(f32[16,4,2,2,2,8,128]{6,5,4,3,2,1,0:T(8,128)} %bitcast_dynamic-update-slice_fusion.2), calls=%async_computation | async-start | bytes 4194304 | tf_op jit(solution)/shard_map/all_to_all | solution.py:57
  39.5 49.2 %all-to-all-done = f32[16,4,2,2,2,8,128]{6,5,4,3,2,1,0:T(8,128)} async-done(((f32[16,4,2,2,2,8,128]{6,5,4,3,2,1,0:T(8,128)}), f32[16,4,2,2,2,8,128]{6,5,4,3,2,1,0:T(8,128)}, u32[]{:S(2)}, u32[]{:S(2)}) %all-to-all-start) | async-done | bytes 2097184 | tf_op jit(solution)/shard_map/all_to_all | solution.py:57
  88.8 1.8 copy_bitcast_fusion.1
  92.3 4.0 %while.52 = (s32[]{:T(128)}, f32[2,2,128,128]{3,2,0,1:T(8,128)S(1)}, f32[2,2,2,128,128]{4,3,1,2,0:T(8,128)}, f32[2,2,2,128,128]{4,3,1,2,0:T(8,128)S(1)}, s32[]{:T(128)}) while((s32[]{:T(128)}, f32[2,2,128,128]{3,2,0,1:T(8,128)S(1)}, f32[2,2,2,128,128]{4,3,1,2,0:T(8,128)}, f32[2,2,2,128,128]{4,3,1,2,0:T(8,128)S(1)}, s32[]{:T(128)}) %tuple.105), condition=%wide.region_5.6_spmd, body=%wide.region_4.5_spmd.sunk | while | flops 201457664 | bytes 7602313 | solution.py:77
  98.3 5.6 %while.50 = (s32[]{:T(128)}, f32[2,2,128,128]{3,2,0,1:T(8,128)S(1)}, f32[3,2,2,128,128]{4,3,1,2,0:T(8,128)}, f32[3,2,2,128,128]{4,3,1,2,0:T(8,128)S(1)}, s32[]{:T(128)}) while((s32[]{:T(128)}, f32[2,2,128,128]{3,2,0,1:T(8,128)S(1)}, f32[3,2,2,128,128]{4,3,1,2,0:T(8,128)}, f32[3,2,2,128,128]{4,3,1,2,0:T(8,128)S(1)}, s32[]{:T(128)}) %tuple.99), condition=%wide.region_1.2_spmd, body=%wide.region_0.1_spmd.sunk | while | flops 201457664 | bytes 3145805 | solution.py:71
  106.1 88.7 %all-gather.7.cloned.1.call-done = f32[64,2,128,128]{3,2,0,1:T(8,128)} async-done(((f32[2,2,128,128]{3,2,0,1:T(8,128)}), f32[64,2,128,128]{3,2,0,1:T(8,128)}) %all-gather.7.cloned.1.call-update) | async-done | bytes 8388624 | tf_op jit(solution)/shard_map/all_gather | solution.py:12
  196.1 102.6 %all-gather.5.cloned.1.call-done = f32[64,2,128,128]{3,2,1,0:T(8,128)} async-done(((f32[2,2,128,128]{3,2,1,0:T(8,128)}), f32[64,2,128,128]{3,2,1,0:T(8,128)}) %all-gather.5.cloned.1.call-update) | async-done | bytes 8388624 | tf_op jit(solution)/shard_map/all_gather | solution.py:12
  298.7 65.7 %while.51 = (s32[]{:T(128)}, f32[2,2,128,128]{3,2,0,1:T(8,128)S(1)}, s32[]{:T(128)}, f32[32,2,2,128,128]{4,3,2,1,0:T(8,128)}, s32[]{:T(128)}, /*index=5*/s32[]{:T(128)}, s32[]{:T(128)}) while((s32[]{:T(128)}, f32[2,2,128,128]{3,2,0,1:T(8,128)S(1)}, s32[]{:T(128)}, f32[32,2,2,128,128]{4,3,2,1,0:T(8,128)}, s32[]{:T(128)}, /*index=5*/s32[]{:T(128)}, ...), condition=%wide.region_3.4_spmd, body=%wide.region_2.3_spmd.sunk | while | flops 201457664 | bytes 2883707 | solution.py:19
  (282 shorter events, 86.5 us)
Async XLA Ops:
  32.2 56.6 %all-to-all-start = ((f32[16,4,2,2,2,8,128]{6,5,4,3,2,1,0:T(8,128)}), f32[16,4,2,2,2,8,128]{6,5,4,3,2,1,0:T(8,128)}, u32[]{:S(2)}, u32[]{:S(2)}) async-start(f32[16,4,2,2,2,8,128]{6,5,4,3,2,1,0:T(8,128)} %bitcast_dynamic-update-slice_fusion.2), calls=%async_computation | async-start | bytes 4194304 | tf_op jit(solution)/shard_map/all_to_all | solution.py:57
  39.5 155.3 %all-gather.7.cloned.1.call-start = ((), (), s32[]{:S(2)}) async-start(), calls=%async_computation.2 | async-start | bytes 8650752 | tf_op jit(solution)/shard_map/all_gather | solution.py:12
  92.3 1.1 copy-start
  93.5 0.8 copy-start.1
  94.3 1.1 copy-start
  95.5 0.8 copy-start.1
  98.1 200.6 %all-gather.5.cloned.1.call-start = ((), (), s32[]{:S(2)}) async-start(), calls=%async_computation.1 | async-start | bytes 8650752 | tf_op jit(solution)/shard_map/all_gather | solution.py:12
  98.2 6.4 %copy-start.4 = (s32[2]{0:T(128)S(1)}, s32[2]{0:T(128)}, u32[]{:S(2)}) copy-start(s32[2]{0:T(128)} %param.11) | copy-start | bytes 28
  98.2 6.5 %copy-start.2 = (f32[2,2,2,128,128]{4,3,1,2,0:T(8,128)S(1)}, f32[2,2,2,128,128]{4,3,1,2,0:T(8,128)}, u32[]{:S(2)}) copy-start(f32[2,2,2,128,128]{4,3,1,2,0:T(8,128)} %get-tuple-element.194) | copy-start | bytes 1572868
  103.9 1.0 copy-start.3
Sparse Core Ops, SparseCore 0:
  98.2 96.4 all-gather.6
  197.9 100.6 all-gather.4
